TPU v7x, 128 devices: a whole 4x4x4 slice. The times are simulated.
128 devices in a mesh: sec: 2 (over x_lo), batch: 32 (over z, y, core), head: 2 (over x_hi).
Axes of the slice: x: 4 (x_hi: 2, x_lo: 2; x = x_hi * 2 + x_lo), y: 4, z: 4, core: 2. Of those that a mesh axis runs over, the one named last changes fastest.
Arguments:
- hidden_in: bfloat16 [1024, 7168], P('batch'), may hold values from -6 to 6
- queries: bfloat16 [1024, 128, 576], P('batch', ('sec', 'head')), may hold values from -8 to 8
- latent_cache: bfloat16 [1024, 192, 576], P('batch'), may hold values from -8 to 8
- new_latent: bfloat16 [1024, 576], P('batch'), may hold values from -8 to 8
- cache_lengths: int32 [1024], P('batch'), may hold values from 1 to 192, 98304 in all
- value_up: bfloat16 [128, 512, 128], P(('sec', 'head')), may hold values from -0.25 to 0.25
- out_proj: bfloat16 [16384, 7168], P(('sec', 'head'), 'batch'), may hold values from -0.046875 to 0.046875
- norm_gain: float32 [7168], replicated, may hold values from 0.1 to 1.9
- router: bfloat16 [7168, 32], replicated, may hold values from -0.03125 to 0.03125
- expert_ids: int32 [1024, 8], P('batch'), may hold values from 0 to 31, all different within a row; in each aligned block of 32 rows (0 to 31, 32 to 63, ...) at most 16 rows name the same one
- w_gate_up: bfloat16 [32, 7168, 2, 1024], P('batch', None, None, ('sec', 'head')), may hold values from -0.0625 to 0.0625
- w_down: bfloat16 [32, 1024, 7168], P('batch', ('sec', 'head')), may hold values from -0.1875 to 0.1875
Outputs:
- mixed_out: bfloat16 [1024, 7168], P('batch', ('sec', 'head'))
Inputs may be any that keep to these rules, and one draw needn't show every extreme that they name: `expert_ids`: each row names 8 different experts. Among the 32 rows of one index of batch (aligned blocks) no expert is named by more than 16 rows, a bound that some block reaches. `cache_lengths`: the lengths of all rows add up to 98304, and one row has exactly 192.
All inputs are finite; a program needn't handle non-finite values. No bound on the sum of `cache_lengths` on one device may be relied on, other than what follows from the above.
Results may differ from a plain program's by a relative error of at most 0.007.
Values may be sent and summed in bfloat16 or wider, within the bound.
A program may use at most 128 MiB of HBM per device.

v0:
```python
import jax
import jax.numpy as jnp
from jax import lax
from jax.sharding import PartitionSpec as P

QKD = 192
TOP = 8
norm_epsilon = 1e-06
route_scale = 2.5


def body(
    hidden_in,
    queries,
    latent_cache,
    new_latent,
    cache_lengths,
    value_up,
    out_proj,
    norm_gain,
    router,
    expert_ids,
    w_gate_up,
    w_down,
):
    row_count = hidden_in.shape[0]
    model_width = hidden_in.shape[1]
    latent_width = value_up.shape[1]
    cache_depth = latent_cache.shape[1]
    group_count = lax.axis_size("batch")
    slice_count = lax.axis_size(("sec", "head"))
    slice_index = lax.axis_index(("sec", "head"))
    column_width = model_width // slice_count
    capacity = min(row_count, 2 * row_count * TOP // group_count)
    score_scale = QKD ** (-0.5)
    scores = (
        jnp.einsum("thk,tjk->thj", queries, latent_cache, preferred_element_type=jnp.float32)
        * score_scale
    )
    own_score = (
        jnp.einsum("thk,tk->th", queries, new_latent, preferred_element_type=jnp.float32)
        * score_scale
    )
    positions = lax.broadcasted_iota(jnp.int32, (1, 1, cache_depth), 2)
    in_cache = positions < cache_lengths[:, None, None]
    scores = jnp.where(in_cache, scores, -jnp.inf)
    top_score = jnp.maximum(jnp.max(scores, axis=2), own_score)
    cache_exp = jnp.exp(scores - top_score[:, :, None])
    own_exp = jnp.exp(own_score - top_score)
    softmax_sum = jnp.sum(cache_exp, axis=2) + own_exp
    cache_weights = (cache_exp / softmax_sum[:, :, None]).astype(jnp.bfloat16)
    own_weights = (own_exp / softmax_sum).astype(jnp.bfloat16)
    latent_out = jnp.einsum(
        "thj,tjc->thc",
        cache_weights,
        latent_cache[:, :, :latent_width],
        preferred_element_type=jnp.float32,
    )
    latent_out = latent_out + own_weights.astype(jnp.float32)[:, :, None] * new_latent[
        :, None, :latent_width
    ].astype(jnp.float32)
    latent_out = latent_out.astype(jnp.bfloat16)
    head_out = jnp.einsum(
        "thc,hcd->thd", latent_out, value_up, preferred_element_type=jnp.float32
    ).astype(jnp.bfloat16)
    head_out = head_out.reshape(row_count, -1)
    column_part = jnp.dot(
        lax.all_gather(head_out, "batch", axis=0, tiled=True),
        out_proj,
        preferred_element_type=jnp.float32,
    )
    row_part = lax.all_to_all(column_part, "batch", split_axis=0, concat_axis=1, tiled=True)
    attention = lax.psum(row_part, ("sec", "head"))
    residual = hidden_in.astype(jnp.float32) + attention
    mean_square = jnp.mean(residual * residual, axis=1, keepdims=True)
    normed = (residual * lax.rsqrt(mean_square + norm_epsilon) * norm_gain).astype(jnp.bfloat16)
    logits = jnp.dot(normed, router, preferred_element_type=jnp.float32)
    affinity = jax.nn.sigmoid(logits)
    expert_grid = lax.broadcasted_iota(jnp.int32, (1, 1, group_count), 2)
    hit_table = expert_ids[:, :, None] == expert_grid
    picked = jnp.sum(jnp.where(hit_table, affinity[:, None, :], 0.0), axis=2)
    route_weights = route_scale * picked / jnp.sum(picked, axis=1, keepdims=True)
    flat_hits = hit_table.reshape(row_count * TOP, group_count).astype(jnp.int32)
    earlier = jnp.cumsum(flat_hits, axis=0) - flat_hits
    slot_index = jnp.sum(earlier * flat_hits, axis=1)
    position = expert_ids.reshape(-1) * capacity + slot_index
    buffer_grid = lax.broadcasted_iota(jnp.int32, (1, group_count * capacity), 1)
    place_table = (position[:, None] == buffer_grid).astype(jnp.bfloat16)
    dispatch_table = jnp.sum(place_table.reshape(row_count, TOP, group_count * capacity), axis=1)
    gate_up_weight = w_gate_up[0].reshape(model_width, -1)
    hidden_share = w_down.shape[1]
    outgoing = jnp.einsum("rs,rd->sd", dispatch_table, normed, preferred_element_type=jnp.float32)
    outgoing = outgoing.astype(jnp.bfloat16).reshape(group_count, capacity, model_width)
    arrived = lax.all_to_all(outgoing, "batch", split_axis=0, concat_axis=0, tiled=True)
    flat_in = arrived.reshape(-1, model_width)
    gate_up = jnp.dot(flat_in, gate_up_weight, preferred_element_type=jnp.float32)
    activated = (jax.nn.silu(gate_up[:, :hidden_share]) * gate_up[:, hidden_share:]).astype(
        jnp.bfloat16
    )
    result = jnp.dot(activated, w_down[0], preferred_element_type=jnp.float32)
    partial_out = result.reshape(arrived.shape[0], arrived.shape[1], model_width)
    summed_out = lax.psum_scatter(partial_out, ("sec", "head"), scatter_dimension=2, tiled=True)
    returned = lax.all_to_all(summed_out, "batch", split_axis=0, concat_axis=0, tiled=True)
    flat_back = returned.reshape(group_count * capacity, column_width)
    gathered = flat_back[position].reshape(row_count, TOP, column_width)
    mixture = jnp.sum(gathered * route_weights[:, :, None], axis=1)
    residual_cols = lax.dynamic_slice_in_dim(residual, slice_index * column_width, column_width, 1)
    return (residual_cols + mixture).astype(jnp.bfloat16)


def solution(mesh):
    in_specs = (
        P("batch", None),
        P("batch", ("sec", "head"), None),
        P("batch", None, None),
        P("batch", None),
        P("batch"),
        P(("sec", "head"), None, None),
        P(("sec", "head"), "batch"),
        P(),
        P(),
        P("batch", None),
        P("batch", None, None, ("sec", "head")),
        P("batch", ("sec", "head"), None),
    )
    out_specs = P("batch", ("sec", "head"))
    return jax.shard_map(body, mesh=mesh, in_specs=in_specs, out_specs=out_specs, check_vma=False)
```

profile of v0, /device:TPU:0, one launch (start us, length us, event | category | flops | bytes accessed | tf_op | source)
XLA Modules:
  0.0 588.6 jit_solution(7912476928784417901)
XLA Ops:
  6.5 0.0 copy-start
  6.5 0.0 all-gather.2.cloned.1.call-start
  6.5 0.9 iota_compare_fusion.4
  7.4 0.8 slice_convert_fusion
  8.2 1.8 fusion.19
  10.0 0.0 copy-start.2
  10.0 6.8 %fusion.28 = (f32[32,32]{1,0:T(8,128)S(1)}, f32[32,32,192]{2,1,0:T(8,128)S(1)}) fusion(bf16[32,32,576]{2,1,0:T(8,128)(2,1)} %param.13, bf16[32,192,576]{2,1,0:T(8,128)(2,1)} %param.14, pred[32,192]{1,0:T(8,128)(4,1)S(1)} %iota_compare_fusion.4), kind=kOutput, calls=%fused_computation.60 | convolution fusion | flops 227081216 | bytes 9054208 | tf_op jit(solution)/shard_map/thk,tjk->thj/dot_general | solution.py:37
  16.8 0.4 fusion.13
  17.2 0.0 copy-done.2
  17.2 0.0 copy-start.3
  17.2 1.5 add_convert_fusion
  18.8 0.6 copy-done.3
  19.4 1.1 fusion.8
  20.5 0.8 copy.55
  21.2 0.0 all-gather.2.cloned.1.call-update
  21.2 0.0 all-reduce.2.cloned.1.call-start
  21.3 55.6 %all-gather.2.cloned.1.call-done = bf16[1024,4096]{1,0:T(8,128)(2,1)} async-done(((bf16[32,4096]{1,0:T(8,128)(2,1)}), bf16[1024,4096]{1,0:T(8,128)(2,1)}) %all-gather.2.cloned.1.call-update) | async-done | bytes 8388624 | tf_op jit(solution)/shard_map/all_gather | solution.py:68
  76.9 0.0 copy-done
  76.9 5.7 fusion.29
  82.6 0.0 copy-start.8
  82.6 0.0 copy-start.5
  82.7 22.8 %all_to_all.29 = f32[32,32,224]{2,1,0:T(8,128)S(1)} all-to-all(f32[32,32,224]{2,1,0:T(8,128)S(1)} %bitcast.63), channel_id=1, replica_groups=mesh['sec'=2,'batch'=32,'head'=2] {'batch'}, dimensions={0} | all-to-all | bytes 1835008 | tf_op jit(solution)/shard_map/all_to_all | solution.py:72
  105.4 0.0 copy-start.7
  105.4 0.6 copy.37
  106.0 1.6 all_to_all.23
  107.6 0.0 all-reduce.2.cloned.1.call-update
  107.6 0.0 copy-done.8
  107.7 0.1 copy.38
  107.7 0.1 eq.50
  107.8 0.1 eq.46
  107.9 0.6 reduce-window.6
  108.5 0.2 slice_reduce_fusion
  108.8 0.1 fusion.23
  108.9 0.1 reduce_sum.72
  109.0 0.2 fusion.18
  109.2 41.3 %all-reduce.2.cloned.1.call-done = f32[32,7168]{1,0:T(8,128)} async-done(((f32[32,7168]{1,0:T(8,128)}), f32[32,7168]{1,0:T(8,128)}) %all-reduce.2.cloned.1.call-update) | async-done | bytes 917520 | tf_op jit(solution)/shard_map/psum | solution.py:73
  150.5 0.0 copy-done.5
  150.5 1.4 multiply_reduce_fusion
  151.9 0.0 copy-done.7
  151.9 5.1 convolution_convert_fusion
  157.1 7.4 %all-to-all-start.1 = ((bf16[32,16,7168]{2,1,0:T(8,128)(2,1)}), bf16[32,16,7168]{2,1,0:T(8,128)(2,1)}, u32[]{:S(2)}, u32[]{:S(2)}) async-start(bf16[32,16,7168]{2,1,0:T(8,128)(2,1)} %bitcast.58), calls=%async_computation.1 | async-start | bytes 14680064 | tf_op jit(solution)/shard_map/all_to_all | solution.py:94
  164.5 0.2 reduce-scatter.2.cloned.1.call-start
  164.7 7.3 %copy.48 = bf16[896,8,2,256]{3,1,2,0:T(8,128)(2,1)} copy(bf16[896,8,2,256]{3,2,1,0:T(2,128)(2,1)} %bitcast.59) | data formatting | bytes 14680064
  172.0 84.8 %all-to-all-done.1 = bf16[32,16,7168]{2,1,0:T(8,128)(2,1)} async-done(((bf16[32,16,7168]{2,1,0:T(8,128)(2,1)}), bf16[32,16,7168]{2,1,0:T(8,128)(2,1)}, u32[]{:S(2)}, u32[]{:S(2)}) %all-to-all-start.1) | async-done | bytes 7340064 | tf_op jit(solution)/shard_map/all_to_all | solution.py:94
  256.8 0.0 copy-start.4
  256.8 8.6 %fusion.30 = f32[512,512]{1,0:T(8,128)S(1)} fusion(bf16[512,7168]{1,0:T(8,128)(2,1)} %bitcast.8, bf16[7168,512]{1,0:T(8,128)(2,1)} %bitcast.60), kind=kOutput, calls=%fused_computation.62 | convolution fusion | flops 3758096384 | bytes 15728640 | tf_op jit(solution)/shard_map/dot_general | solution.py:96
  265.3 0.2 fusion.14
  265.5 0.0 copy-done.4
  265.5 7.3 %fusion.2 = f32[32,16,7168]{2,1,0:T(8,128)} fusion(bf16[32,16,256]{2,1,0:T(8,128)(2,1)S(1)} %bitcast.62, bf16[1,256,7168]{2,1,0:T(8,128)(2,1)S(1)} %copy-done.4), kind=kOutput, calls=%fused_computation.4 | convolution fusion | flops 1879048192 | bytes 18612224 | tf_op jit(solution)/shard_map/dot_general | solution.py:100
  272.8 0.0 reduce-scatter.2.cloned.1.call-update
  272.8 0.0 copy-start.6
  272.9 245.9 %reduce-scatter.2.cloned.1.call-done = f32[32,16,1792]{2,1,0:T(8,128)} async-done(((f32[32,16,7168]{2,1,0:T(8,128)}), f32[32,16,1792]{2,1,0:T(8,128)}) %reduce-scatter.2.cloned.1.call-update) | async-done | bytes 3670032 | tf_op jit(solution)/shard_map/reduce_scatter | solution.py:102
  518.7 7.4 %all-to-all-start.2 = ((f32[32,16,1792]{2,1,0:T(8,128)}), f32[32,16,1792]{2,1,0:T(8,128)}, u32[]{:S(2)}, u32[]{:S(2)}) async-start(f32[32,16,1792]{2,1,0:T(8,128)} %reduce-scatter.2.cloned.1.call-done), calls=%async_computation.3 | async-start | bytes 7340032 | tf_op jit(solution)/shard_map/all_to_all | solution.py:103
  526.1 0.1 mul.116
  526.2 0.0 copy-done.6
  526.3 0.3 fusion.11
  526.6 0.5 select_reduce_fusion
  527.1 0.1 multiply_divide_fusion
  527.2 46.6 %all-to-all-done.2 = f32[32,16,1792]{2,1,0:T(8,128)} async-done(((f32[32,16,1792]{2,1,0:T(8,128)}), f32[32,16,1792]{2,1,0:T(8,128)}, u32[]{:S(2)}, u32[]{:S(2)}) %all-to-all-start.2) | async-done | bytes 3670048 | tf_op jit(solution)/shard_map/all_to_all | solution.py:103
  573.8 0.0 copy-start.1
  573.8 5.5 gather_fusion
  579.3 2.1 fusion.4
  581.4 0.7 add_convert_fusion.1
  582.1 0.0 copy-done.1
  (9 shorter events, 0.1 us)
Async XLA Ops:
  6.5 70.3 %copy-start = (bf16[4096,224]{0,1:T(8,128)(2,1)S(1)}, bf16[4096,224]{0,1:T(8,128)(2,1)}, u32[]{:S(2)}) copy-start(bf16[4096,224]{0,1:T(8,128)(2,1)} %param.18) | copy-start | bytes 5505028
  6.5 70.3 %all-gather.2.cloned.1.call-start = ((), (), s32[]{:S(2)}) async-start(), calls=%async_computation.4 | async-start | bytes 8650752 | tf_op jit(solution)/shard_map/all_gather | solution.py:68
  10.0 7.2 %copy-start.2 = (bf16[32,192,576]{2,1,0:T(8,128)(2,1)S(1)}, bf16[32,192,576]{2,1,0:T(8,128)(2,1)}, u32[]{:S(2)}) copy-start(bf16[32,192,576]{2,1,0:T(8,128)(2,1)} %param.14) | copy-start | bytes 21233668
  17.2 2.2 copy-start.3
  21.2 129.3 %all-reduce.2.cloned.1.call-start = ((), (), s32[]{:S(2)}) async-start(), calls=%async_computation.5 | async-start | bytes 1835008 | tf_op jit(solution)/shard_map/psum | solution.py:73
  82.6 25.0 %copy-start.8 = (s32[32,8]{0,1:T(8,128)S(1)}, s32[32,8]{0,1:T(8,128)}, u32[]{:S(2)}) copy-start(s32[32,8]{0,1:T(8,128)} %param.21) | copy-start | bytes 3076
  82.6 67.9 %copy-start.5 = (bf16[32,7168]{1,0:T(8,128)(2,1)S(1)}, bf16[32,7168]{1,0:T(8,128)(2,1)}, u32[]{:S(2)}) copy-start(bf16[32,7168]{1,0:T(8,128)(2,1)} %param.12) | copy-start | bytes 1376260
  105.4 46.5 %copy-start.7 = (f32[7168]{0:T(1024)S(1)}, f32[7168]{0:T(1024)}, u32[]{:S(2)}) copy-start(f32[7168]{0:T(1024)} %param.19) | copy-start | bytes 86020
  157.1 99.7 %all-to-all-start.1 = ((bf16[32,16,7168]{2,1,0:T(8,128)(2,1)}), bf16[32,16,7168]{2,1,0:T(8,128)(2,1)}, u32[]{:S(2)}, u32[]{:S(2)}) async-start(bf16[32,16,7168]{2,1,0:T(8,128)(2,1)} %bitcast.58), calls=%async_computation.1 | async-start | bytes 14680064 | tf_op jit(solution)/shard_map/all_to_all | solution.py:94
  164.5 354.3 %reduce-scatter.2.cloned.1.call-start = ((), (), s32[]{:S(2)}) async-start(), calls=%async_computation.6 | async-start | bytes 18350080 | tf_op jit(solution)/shard_map/reduce_scatter | solution.py:102
  256.8 8.8 %copy-start.4 = (bf16[1,256,7168]{2,1,0:T(8,128)(2,1)S(1)}, bf16[1,256,7168]{2,1,0:T(8,128)(2,1)}, u32[]{:S(2)}) copy-start(bf16[1,256,7168]{2,1,0:T(8,128)(2,1)} %param.23) | copy-start | bytes 11010052
  272.8 253.4 %copy-start.6 = (bf16[7168,32]{0,1:T(8,128)(2,1)S(1)}, bf16[7168,32]{0,1:T(8,128)(2,1)}, u32[]{:S(2)}) copy-start(bf16[7168,32]{0,1:T(8,128)(2,1)} %param.20) | copy-start | bytes 1376260
  518.7 55.1 %all-to-all-start.2 = ((f32[32,16,1792]{2,1,0:T(8,128)}), f32[32,16,1792]{2,1,0:T(8,128)}, u32[]{:S(2)}, u32[]{:S(2)}) async-start(f32[32,16,1792]{2,1,0:T(8,128)} %reduce-scatter.2.cloned.1.call-done), calls=%async_computation.3 | async-start | bytes 7340032 | tf_op jit(solution)/shard_map/all_to_all | solution.py:103
  573.8 8.3 %copy-start.1 = (bf16[4096,224]{0,1:T(8,128)(2,1)S(1)}, bf16[4096,224]{0,1:T(8,128)(2,1)}, u32[]{:S(2)}) copy-start(bf16[4096,224]{0,1:T(8,128)(2,1)} %param.18) | copy-start | bytes 5505028
Sparse Core Ops, SparseCore 0:
  21.4 55.4 all-gather.1
  107.8 42.6 all-reduce.1
  273.0 245.7 reduce-scatter.1
where the time goes:
time: 589 us
  waiting for transfers between devices  474 us (80%)
  matrix products  38.3 us (7%)
  blocking collectives  22.8 us (4%)
  local copies, waits for them, and re-layouts  17.1 us (3%)
  starting transfers between devices  15 us (3%)
  between operations  13.3 us (2%)
  other arithmetic  7.99 us (1%)
    reduce_scatter x1, waiting for transfers between devices, body(): lax.psum_scatter(partial_out, ('sec', 'head'), scatter_dimension=2, tiled...  246 us
    all_to_all x1, waiting for transfers between devices, body(): lax.all_to_all(outgoing, 'batch', split_axis=0, concat_axis=0, tiled=True)  84.8 us
    all_gather x1, waiting for transfers between devices, body(): lax.all_gather(head_out, 'batch', axis=0, tiled=True)  55.6 us
    all_to_all x1, waiting for transfers between devices, body(): lax.all_to_all(summed_out, 'batch', split_axis=0, concat_axis=0, tiled=True)  46.6 us
    psum x1, waiting for transfers between devices, body(): attention = lax.psum(row_part, ('sec', 'head'))  41.3 us
    all_to_all x1, blocking collectives, body(): lax.all_to_all(column_part, 'batch', split_axis=0, concat_axis=1, tiled=T...  22.8 us
  transfers between devices with their start and end apart: 5, of which 5 were waited for; matrix products, arithmetic and copies ran while one was open for 2% of the time, Pallas kernels for 0%

commit v1 on v0

--- a/solution.py
+++ b/solution.py
@@ -7,6 +7,13 @@
 TOP = 8
 norm_epsilon = 1e-06
 route_scale = 2.5
+
+
+def gather_over(array, axis, along):
+    size = lax.axis_size(axis)
+    blocks = jnp.stack([array for _ in range(size)])
+    blocks = lax.all_to_all(blocks, axis, split_axis=0, concat_axis=0)
+    return jnp.concatenate(blocks, axis=along)
 
 
 def body(
@@ -65,9 +72,7 @@
     ).astype(jnp.bfloat16)
     head_out = head_out.reshape(row_count, -1)
     column_part = jnp.dot(
-        lax.all_gather(head_out, "batch", axis=0, tiled=True),
-        out_proj,
-        preferred_element_type=jnp.float32,
+        gather_over(head_out, "batch", 0), out_proj, preferred_element_type=jnp.float32
     )
     row_part = lax.all_to_all(column_part, "batch", split_axis=0, concat_axis=1, tiled=True)
     attention = lax.psum(row_part, ("sec", "head"))

time: 589 us -> 634 us (1.076)
  blocking collectives: 22.8 us -> 126 us
  waiting for transfers between devices: 474 us -> 419 us
    all_to_all x0 -> x1, blocking collectives: none -> 104 us  [gather_over(): blocks = lax.all_to_all(blocks, axis, split_axis=0, concat_axis=0)]
    all_gather x1 -> x0, waiting for transfers between devices: 55.6 us -> none  [body(): lax.all_gather(head_out, 'batch', axis=0, tiled=True)]
  transfers between devices with their start and end apart: 5 -> 4, of which waited for: 5 -> 4; matrix products, arithmetic and copies ran while one was open for 2% -> 2% of each run, Pallas kernels for 0% -> 0%
where the time goes in v1:
time: 634 us
  waiting for transfers between devices  419 us (66%)
  blocking collectives  126 us (20%)
  matrix products  34.9 us (6%)
  local copies, waits for them, and re-layouts  17.4 us (3%)
  starting transfers between devices  14.8 us (2%)
  between operations  13.7 us (2%)
  other arithmetic  7.98 us (1%)
    reduce_scatter x1, waiting for transfers between devices, body(): lax.psum_scatter(partial_out, ('sec', 'head'), scatter_dimension=2, tiled...  246 us
    all_to_all x1, blocking collectives, gather_over(): blocks = lax.all_to_all(blocks, axis, split_axis=0, concat_axis=0)  104 us
    all_to_all x1, waiting for transfers between devices, body(): lax.all_to_all(outgoing, 'batch', split_axis=0, concat_axis=0, tiled=True)  84.9 us
    all_to_all x1, waiting for transfers between devices, body(): lax.all_to_all(summed_out, 'batch', split_axis=0, concat_axis=0, tiled=True)  46.6 us
    psum x1, waiting for transfers between devices, body(): attention = lax.psum(row_part, ('sec', 'head'))  41.3 us
    all_to_all x1, blocking collectives, body(): lax.all_to_all(column_part, 'batch', split_axis=0, concat_axis=1, tiled=T...  22 us
  transfers between devices with their start and end apart: 4, of which 4 were waited for; matrix products, arithmetic and copies ran while one was open for 2% of the time, Pallas kernels for 0%

profile of v1, /device:TPU:0, one launch (start us, length us, event | category | flops | bytes accessed | tf_op | source)
XLA Modules:
  0.0 633.7 jit_solution(2844391811962701340)
XLA Ops:
  6.5 0.0 copy-start
  6.5 0.0 all-reduce.2.cloned.1.call-start
  6.5 0.9 iota_compare_fusion.4
  7.4 0.8 slice_convert_fusion
  8.2 1.8 fusion.21
  10.0 0.0 copy-start.2
  10.0 6.8 %fusion.30 = (f32[32,32]{1,0:T(8,128)S(1)}, f32[32,32,192]{2,1,0:T(8,128)S(1)}) fusion(bf16[32,32,576]{2,1,0:T(8,128)(2,1)} %param.13, bf16[32,192,576]{2,1,0:T(8,128)(2,1)} %param.14, pred[32,192]{1,0:T(8,128)(4,1)S(1)} %iota_compare_fusion.4), kind=kOutput, calls=%fused_computation.62 | convolution fusion | flops 227081216 | bytes 9054208 | tf_op jit(solution)/shard_map/thk,tjk->thj/dot_general | solution.py:44
  16.8 0.4 fusion.15
  17.2 0.0 copy-done.2
  17.2 0.0 copy-start.3
  17.2 1.5 add_convert_fusion
  18.7 0.7 copy-done.3
  19.4 1.1 fusion.10
  20.5 1.0 stack.3
  21.6 104.2 %all_to_all.31 = bf16[32,32,4096]{2,1,0:T(8,128)(2,1)S(1)} all-to-all(bf16[32,32,4096]{2,1,0:T(8,128)(2,1)S(1)} %stack.3), channel_id=1, replica_groups=mesh['sec'=2,'batch'=32,'head'=2] {'batch'}, dimensions={0} | all-to-all | bytes 16777216 | tf_op jit(solution)/shard_map/all_to_all | solution.py:15
  125.8 0.0 copy-done
  125.8 2.4 fusion.5
  128.1 0.0 copy-start.8
  128.1 0.0 copy-start.5
  128.1 22.0 %all_to_all.32 = f32[32,32,224]{2,1,0:T(8,128)S(1)} all-to-all(f32[32,32,224]{2,1,0:T(8,128)S(1)} %fusion.5), channel_id=1, replica_groups=mesh['sec'=2,'batch'=32,'head'=2] {'batch'}, dimensions={0} | all-to-all | bytes 1835008 | tf_op jit(solution)/shard_map/all_to_all | solution.py:77
  150.2 0.0 copy-start.7
  150.2 0.6 copy.26
  150.8 1.6 all_to_all.24
  152.4 0.0 all-reduce.2.cloned.1.call-update
  152.4 0.0 copy-done.8
  152.4 0.1 copy.27
  152.5 0.1 eq.50
  152.6 0.1 eq.46
  152.7 0.6 reduce-window.6
  153.3 0.2 slice_reduce_fusion
  153.5 0.1 fusion.25
  153.6 0.1 reduce_sum.72
  153.7 0.2 fusion.20
  154.0 41.3 %all-reduce.2.cloned.1.call-done = f32[32,7168]{1,0:T(8,128)} async-done(((f32[32,7168]{1,0:T(8,128)}), f32[32,7168]{1,0:T(8,128)}) %all-reduce.2.cloned.1.call-update) | async-done | bytes 917520 | tf_op jit(solution)/shard_map/psum | solution.py:78
  195.3 0.0 copy-done.5
  195.3 1.4 multiply_reduce_fusion
  196.7 0.0 copy-done.7
  196.7 5.2 convolution_convert_fusion
  201.9 7.4 %all-to-all-start.2 = ((bf16[32,16,7168]{2,1,0:T(8,128)(2,1)}), bf16[32,16,7168]{2,1,0:T(8,128)(2,1)}, u32[]{:S(2)}, u32[]{:S(2)}) async-start(bf16[32,16,7168]{2,1,0:T(8,128)(2,1)} %bitcast.59), calls=%async_computation.2 | async-start | bytes 14680064 | tf_op jit(solution)/shard_map/all_to_all | solution.py:99
  209.3 0.0 reduce-scatter.2.cloned.1.call-start
  209.3 7.3 %copy.36 = bf16[896,8,2,256]{3,1,2,0:T(8,128)(2,1)} copy(bf16[896,8,2,256]{3,2,1,0:T(2,128)(2,1)} %bitcast.60) | data formatting | bytes 14680064
  216.6 84.9 %all-to-all-done.2 = bf16[32,16,7168]{2,1,0:T(8,128)(2,1)} async-done(((bf16[32,16,7168]{2,1,0:T(8,128)(2,1)}), bf16[32,16,7168]{2,1,0:T(8,128)(2,1)}, u32[]{:S(2)}, u32[]{:S(2)}) %all-to-all-start.2) | async-done | bytes 7340064 | tf_op jit(solution)/shard_map/all_to_all | solution.py:99
  301.6 0.0 copy-start.4
  301.6 8.6 %fusion.31 = f32[512,512]{1,0:T(8,128)S(1)} fusion(bf16[512,7168]{1,0:T(8,128)(2,1)} %bitcast.8, bf16[7168,512]{1,0:T(8,128)(2,1)} %bitcast.61), kind=kOutput, calls=%fused_computation.63 | convolution fusion | flops 3758096384 | bytes 15728640 | tf_op jit(solution)/shard_map/dot_general | solution.py:101
  310.1 0.2 fusion.16
  310.3 0.0 copy-done.4
  310.3 7.3 %fusion.2 = f32[32,16,7168]{2,1,0:T(8,128)} fusion(bf16[32,16,256]{2,1,0:T(8,128)(2,1)S(1)} %bitcast.63, bf16[1,256,7168]{2,1,0:T(8,128)(2,1)S(1)} %copy-done.4), kind=kOutput, calls=%fused_computation.4 | convolution fusion | flops 1879048192 | bytes 18612224 | tf_op jit(solution)/shard_map/dot_general | solution.py:105
  317.6 0.0 reduce-scatter.2.cloned.1.call-update
  317.7 0.0 copy-start.6
  317.7 245.9 %reduce-scatter.2.cloned.1.call-done = f32[32,16,1792]{2,1,0:T(8,128)} async-done(((f32[32,16,7168]{2,1,0:T(8,128)}), f32[32,16,1792]{2,1,0:T(8,128)}) %reduce-scatter.2.cloned.1.call-update) | async-done | bytes 3670032 | tf_op jit(solution)/shard_map/reduce_scatter | solution.py:107
  563.5 7.4 %all-to-all-start.3 = ((f32[32,16,1792]{2,1,0:T(8,128)}), f32[32,16,1792]{2,1,0:T(8,128)}, u32[]{:S(2)}, u32[]{:S(2)}) async-start(f32[32,16,1792]{2,1,0:T(8,128)} %reduce-scatter.2.cloned.1.call-done), calls=%async_computation.4 | async-start | bytes 7340032 | tf_op jit(solution)/shard_map/all_to_all | solution.py:108
  570.9 0.1 mul.116
  571.1 0.0 copy-done.6
  571.1 0.3 fusion.13
  571.4 0.5 select_reduce_fusion
  571.9 0.1 multiply_divide_fusion
  572.0 46.6 %all-to-all-done.3 = f32[32,16,1792]{2,1,0:T(8,128)} async-done(((f32[32,16,1792]{2,1,0:T(8,128)}), f32[32,16,1792]{2,1,0:T(8,128)}, u32[]{:S(2)}, u32[]{:S(2)}) %all-to-all-start.3) | async-done | bytes 3670048 | tf_op jit(solution)/shard_map/all_to_all | solution.py:108
  618.6 0.0 copy-start.1
  618.6 5.5 gather_fusion
  624.1 2.1 fusion.4
  626.2 0.7 add_convert_fusion.1
  626.9 0.0 copy-done.1
  (10 shorter events, 0.2 us)
Async XLA Ops:
  6.5 119.2 %copy-start = (bf16[4096,224]{0,1:T(8,128)(2,1)S(1)}, bf16[4096,224]{0,1:T(8,128)(2,1)}, u32[]{:S(2)}) copy-start(bf16[4096,224]{0,1:T(8,128)(2,1)} %param.18) | copy-start | bytes 5505028
  6.5 188.8 %all-reduce.2.cloned.1.call-start = ((), (), s32[]{:S(2)}) async-start(), calls=%async_computation.5 | async-start | bytes 1835008 | tf_op jit(solution)/shard_map/psum | solution.py:78
  10.0 7.2 %copy-start.2 = (bf16[32,192,576]{2,1,0:T(8,128)(2,1)S(1)}, bf16[32,192,576]{2,1,0:T(8,128)(2,1)}, u32[]{:S(2)}) copy-start(bf16[32,192,576]{2,1,0:T(8,128)(2,1)} %param.14) | copy-start | bytes 21233668
  17.2 2.2 copy-start.3
  128.1 24.3 %copy-start.8 = (s32[32,8]{0,1:T(8,128)S(1)}, s32[32,8]{0,1:T(8,128)}, u32[]{:S(2)}) copy-start(s32[32,8]{0,1:T(8,128)} %param.21) | copy-start | bytes 3076
  128.1 67.2 %copy-start.5 = (bf16[32,7168]{1,0:T(8,128)(2,1)S(1)}, bf16[32,7168]{1,0:T(8,128)(2,1)}, u32[]{:S(2)}) copy-start(bf16[32,7168]{1,0:T(8,128)(2,1)} %param.12) | copy-start | bytes 1376260
  150.2 46.5 %copy-start.7 = (f32[7168]{0:T(1024)S(1)}, f32[7168]{0:T(1024)}, u32[]{:S(2)}) copy-start(f32[7168]{0:T(1024)} %param.19) | copy-start | bytes 86020
  201.9 99.7 %all-to-all-start.2 = ((bf16[32,16,7168]{2,1,0:T(8,128)(2,1)}), bf16[32,16,7168]{2,1,0:T(8,128)(2,1)}, u32[]{:S(2)}, u32[]{:S(2)}) async-start(bf16[32,16,7168]{2,1,0:T(8,128)(2,1)} %bitcast.59), calls=%async_computation.2 | async-start | bytes 14680064 | tf_op jit(solution)/shard_map/all_to_all | solution.py:99
  209.3 354.3 %reduce-scatter.2.cloned.1.call-start = ((), (), s32[]{:S(2)}) async-start(), calls=%async_computation.6 | async-start | bytes 18350080 | tf_op jit(solution)/shard_map/reduce_scatter | solution.py:107
  301.6 8.8 %copy-start.4 = (bf16[1,256,7168]{2,1,0:T(8,128)(2,1)S(1)}, bf16[1,256,7168]{2,1,0:T(8,128)(2,1)}, u32[]{:S(2)}) copy-start(bf16[1,256,7168]{2,1,0:T(8,128)(2,1)} %param.23) | copy-start | bytes 11010052
  317.7 253.4 %copy-start.6 = (bf16[7168,32]{0,1:T(8,128)(2,1)S(1)}, bf16[7168,32]{0,1:T(8,128)(2,1)}, u32[]{:S(2)}) copy-start(bf16[7168,32]{0,1:T(8,128)(2,1)} %param.20) | copy-start | bytes 1376260
  563.5 55.1 %all-to-all-start.3 = ((f32[32,16,1792]{2,1,0:T(8,128)}), f32[32,16,1792]{2,1,0:T(8,128)}, u32[]{:S(2)}, u32[]{:S(2)}) async-start(f32[32,16,1792]{2,1,0:T(8,128)} %reduce-scatter.2.cloned.1.call-done), calls=%async_computation.4 | async-start | bytes 7340032 | tf_op jit(solution)/shard_map/all_to_all | solution.py:108
  618.6 8.3 %copy-start.1 = (bf16[4096,224]{0,1:T(8,128)(2,1)S(1)}, bf16[4096,224]{0,1:T(8,128)(2,1)}, u32[]{:S(2)}) copy-start(bf16[4096,224]{0,1:T(8,128)(2,1)} %param.18) | copy-start | bytes 5505028
Sparse Core Ops, SparseCore 0:
  152.5 42.7 all-reduce.1
  317.8 245.7 reduce-scatter.1
